TPU v7x, 32 devices: a whole 2x2x4 slice. The times are simulated.
32 devices in a mesh: section: 2 (over x), expert: 16 (over z, y, core).
Axes of the slice: x: 2, y: 2, z: 4, core: 2. Of those that a mesh axis runs over, the one named last changes fastest.
Arguments:
- tokens: bfloat16 [4, 512, 2048], P(None, 'expert'), may hold values from -6 to 6
- attn_norm: float32 [2, 2048], P('section'), may hold values from 0.5 to 2
- moe_norm: float32 [2, 2048], P('section'), may hold values from 0.5 to 2
- query_weight: bfloat16 [2, 2048, 1024], P('section', 'expert'), may hold values from -4 to 4
- key_weight: bfloat16 [2, 2048, 128], P('section', 'expert'), may hold values from -0.125 to 0.125
- value_weight: bfloat16 [2, 2048, 128], P('section', 'expert'), may hold values from -0.125 to 0.125
- out_weight: bfloat16 [2, 1024, 2048], P('section', 'expert'), may hold values from -0.1875 to 0.1875
- gate_proj: bfloat16 [2, 16, 2048, 704], P('section', 'expert'), may hold values from -0.125 to 0.125
- up_proj: bfloat16 [2, 16, 2048, 704], P('section', 'expert'), may hold values from -0.125 to 0.125
- down_proj: bfloat16 [2, 16, 704, 2048], P('section', 'expert'), may hold values from -0.21875 to 0.21875
- routes: int32 [2, 4, 512, 6], P('section', None, 'expert'), may hold values from 0 to 15, all different within a row; in each aligned block of 32 rows (0 to 31, 32 to 63, ..., all dimensions but the last counted through in order) at most 16 rows name the same one
- weights_code: int32 [2, 4, 512, 6], P('section', None, 'expert'), may hold values from 8 to 64
Outputs:
- hidden_states: bfloat16 [2, 4, 512, 2048], P('section', None, 'expert')
Inputs may be any that keep to these rules, and one draw needn't show every extreme that they name: `routes`: each row names 6 different experts. In each aligned block of 32 rows (one sequence's tokens of one micro-batch of one layer) no expert is named by more than 16 rows, a bound that some block reaches.
All inputs are finite; a program needn't handle non-finite values.
Results may differ from a plain program's by a relative error of at most 0.03.
Values may be sent and summed in bfloat16 or wider, within the bound.
A program may use at most 128 MiB of HBM per device.

v0:
```python
import jax
import jax.numpy as jnp
from jax import lax
from jax.sharding import PartitionSpec as P

epsilon = 1e-06


def shifted(value, axis, steps):
    count = lax.axis_size(axis)
    initial, last = (max(0, -steps), min(count, count - steps))
    return lax.ppermute(value, axis, [(source, source + steps) for source in range(initial, last)])


def rms_scale(features, gain_vector):
    return (
        features
        * lax.rsqrt(jnp.mean(features * features, axis=-1, keepdims=True) + epsilon)
        * gain_vector
    )


def expert_rows(slot_rows, gate_matrix, up_matrix, down_matrix):
    gated = jnp.dot(slot_rows, gate_matrix, preferred_element_type=jnp.float32)
    lifted = jnp.dot(slot_rows, up_matrix, preferred_element_type=jnp.float32)
    hidden = (jax.nn.silu(gated) * lifted).astype(jnp.bfloat16)
    return jnp.dot(hidden, down_matrix, preferred_element_type=jnp.float32).astype(jnp.bfloat16)


def route_tables(picks_block, codes_block, expert_count, capacity, member, members):
    tok_rows, pick_count = picks_block.shape
    flat_ids = picks_block.reshape(-1)
    matches = (flat_ids[:, None] == jnp.arange(expert_count, dtype=jnp.int32)[None, :]).astype(
        jnp.int32
    )
    slot_ranks = jnp.sum((jnp.cumsum(matches, axis=0) - matches) * matches, axis=1)
    columns = (flat_ids * members + member) * capacity + slot_ranks
    capacity = members * capacity
    onehot = (
        columns[:, None] == jnp.arange(expert_count * capacity, dtype=jnp.int32)[None, :]
    ).astype(jnp.float32)
    onehot = onehot.reshape(tok_rows, pick_count, expert_count * capacity)
    scatter_table = jnp.sum(onehot, axis=1).astype(jnp.bfloat16)
    pick_weights = codes_block.astype(jnp.float32) / 64.0
    combine_table = jnp.sum(onehot * pick_weights[:, :, None], axis=1).astype(jnp.bfloat16)
    return (scatter_table, combine_table)


def shards(
    tokens,
    attn_norm,
    moe_norm,
    query_weight,
    key_weight,
    value_weight,
    out_weight,
    gate_proj,
    up_proj,
    down_proj,
    routes,
    weights_code,
):
    section_count = lax.axis_size("section")
    section_index = lax.axis_index("section")
    expert_devices = lax.axis_size("expert")
    micro_count, tok_rows, model_width = tokens.shape
    pick_count = routes.shape[3]
    expert_count = expert_devices * gate_proj.shape[1]
    capacity = min(tok_rows, tok_rows * pick_count * 4 // (3 * expert_count))
    head_size = key_weight.shape[-1]
    head_count = query_weight.shape[-1] // head_size
    full_mixed = lax.all_gather(
        jnp.concatenate([query_weight[0], key_weight[0], value_weight[0]], axis=-1),
        "expert",
        axis=0,
        tiled=True,
    )
    full_out = lax.all_gather(out_weight[0], "expert", axis=0, tiled=True)
    members = 2 if section_count <= 2 and micro_count % 2 == 0 else 1
    group_count, block_rows = micro_count // members, members * tok_rows
    lag = 1
    score_scale = head_size ** (-0.5)
    attn_gain = attn_norm[0]
    moe_gain = moe_norm[0]
    gate_matrix = gate_proj[0, 0]
    up_matrix = up_proj[0, 0]
    down_matrix = down_proj[0, 0]
    group_slots = members * capacity

    def member_tables(picks, codes, member):
        return route_tables(picks, codes, expert_count, capacity, member, members)

    scatter_tables, combine_tables = jax.vmap(member_tables)(
        routes[0], weights_code[0], jnp.arange(micro_count, dtype=jnp.int32) % members
    )
    scatter_tables = scatter_tables.reshape(group_count, block_rows, -1)
    combine_tables = combine_tables.reshape(group_count, block_rows, -1)
    token_groups = tokens.reshape(group_count, block_rows, model_width)

    def attend(wide_input, tick, keys, values):
        normed = rms_scale(wide_input, attn_gain).astype(jnp.bfloat16)
        projected = jnp.dot(normed, full_mixed, preferred_element_type=jnp.float32).astype(
            jnp.bfloat16
        )
        query_rows = projected[:, : head_count * head_size].reshape(
            block_rows, head_count, head_size
        )
        keys.append(projected[:, head_count * head_size : (head_count + 1) * head_size])
        values.append(projected[:, (head_count + 1) * head_size :])
        oldest = max(0, tick + 1 - group_count)
        key_vectors = jnp.concatenate(keys[oldest:], axis=0)
        value_vectors = jnp.concatenate(values[oldest:], axis=0)
        attention_scores = (
            jnp.einsum("qhd,kd->hqk", query_rows, key_vectors, preferred_element_type=jnp.float32)
            * score_scale
        )
        span = (tick + 1 - oldest) * block_rows
        places = jnp.arange(span, dtype=jnp.int32)[None, :] + oldest * block_rows
        query_places = tick * block_rows + jnp.arange(block_rows, dtype=jnp.int32)[:, None]
        causal = (places <= query_places) & (
            (places >= lag * section_index * block_rows) | (places == query_places)
        )
        attention_scores = jnp.where(causal[None], attention_scores, -1e30)
        highest = jnp.max(attention_scores, axis=-1, keepdims=True)
        exponent = jnp.exp(attention_scores - highest)
        attention_probabilities = (exponent / jnp.sum(exponent, axis=-1, keepdims=True)).astype(
            jnp.bfloat16
        )
        attended_values = jnp.einsum(
            "hqk,kd->qhd",
            attention_probabilities,
            value_vectors,
            preferred_element_type=jnp.float32,
        )
        attended_values = attended_values.astype(jnp.bfloat16).reshape(
            block_rows, head_count * head_size
        )
        return jnp.dot(attended_values, full_out, preferred_element_type=jnp.float32)

    def mixture(wide_input, scatter_table, combine_table):
        moe_input = rms_scale(wide_input, moe_gain).astype(jnp.bfloat16)
        outgoing = jnp.einsum(
            "te,td->ed", scatter_table, moe_input, preferred_element_type=jnp.float32
        )
        outgoing = outgoing.astype(jnp.bfloat16).reshape(expert_count, group_slots, model_width)
        arrived = lax.all_to_all(outgoing, "expert", split_axis=0, concat_axis=0, tiled=True)
        produced = expert_rows(
            arrived.reshape(-1, model_width), gate_matrix, up_matrix, down_matrix
        ).reshape(arrived.shape)
        returned = lax.all_to_all(produced, "expert", split_axis=0, concat_axis=0, tiled=True)
        return jnp.dot(
            combine_table, returned.reshape(-1, model_width), preferred_element_type=jnp.float32
        )

    keys, values, results, inbound = [], [], [], []
    for tick in range(group_count + lag * (section_count - 1)):
        clipped = jnp.clip(tick - lag * section_index, 0, group_count - 1)
        layer_input = token_groups[min(tick, group_count - 1)]
        if tick >= lag:
            layer_input = jnp.where(section_index == 0, layer_input, inbound[tick - lag])
        wide_input = layer_input.astype(jnp.float32)
        mixed = mixture(
            wide_input,
            lax.dynamic_index_in_dim(scatter_tables, clipped, 0, keepdims=False),
            lax.dynamic_index_in_dim(combine_tables, clipped, 0, keepdims=False),
        )
        attended = attend(wide_input, tick, keys, values)
        results.append((wide_input + attended + mixed).astype(jnp.bfloat16))
        if tick + lag < group_count + lag * (section_count - 1):
            inbound.append(shifted(results[-1], "section", 1))
    stacked = jnp.stack(results)
    chosen = lax.dynamic_slice_in_dim(stacked, lag * section_index, group_count, 0)
    return chosen.reshape(1, micro_count, tok_rows, model_width)


def solution(mesh):
    placed = (
        P(None, "expert", None),
        P("section", None),
        P("section", None),
        P("section", "expert", None),
        P("section", "expert", None),
        P("section", "expert", None),
        P("section", "expert", None),
        P("section", "expert", None, None),
        P("section", "expert", None, None),
        P("section", "expert", None, None),
        P("section", None, "expert", None),
        P("section", None, "expert", None),
    )
    return jax.shard_map(
        shards,
        mesh=mesh,
        in_specs=placed,
        out_specs=P("section", None, "expert", None),
        check_vma=False,
    )
```

profile of v0, /device:TPU:15, one launch (start us, length us, event | category | flops | bytes accessed | tf_op | source)
XLA Modules:
  0.0 473.2 jit_solution(7289578569801353068)
XLA Ops:
  6.5 1.9 pad_maximum_fusion
  8.5 0.8 copy.38
  9.4 0.6 copy_bitcast_fusion
  10.0 4.2 reduce-window.6
  14.2 0.7 slice.62
  14.9 1.0 copy.41
  16.0 0.7 reduce_sum.98
  16.8 0.9 fusion.146
  17.7 0.7 copy.44
  18.4 0.7 multiply_bitcast_fusion
  19.1 0.6 copy.45
  19.8 1.1 select_reduce_fusion
  21.0 0.6 copy-done.18
  21.7 2.1 convolution_convert_fusion.5
  23.8 6.5 %all-to-all-start = ((bf16[16,32,2048]{2,1,0:T(8,128)(2,1)}), bf16[16,32,2048]{2,1,0:T(8,128)(2,1)}, u32[]{:S(2)}, u32[]{:S(2)}) async-start(bf16[16,32,2048]{2,1,0:T(8,128)(2,1)} %bitcast.317), calls=%async_computation | async-start | bytes 4194304 | tf_op jit(solution)/shard_map/all_to_all | solution.py:146
  30.3 0.7 all-gather.6.cloned.1.call-update
  31.0 68.3 %all-to-all-done = bf16[16,32,2048]{2,1,0:T(8,128)(2,1)} async-done(((bf16[16,32,2048]{2,1,0:T(8,128)(2,1)}), bf16[16,32,2048]{2,1,0:T(8,128)(2,1)}, u32[]{:S(2)}, u32[]{:S(2)}) %all-to-all-start) | async-done | bytes 2097184 | tf_op jit(solution)/shard_map/all_to_all | solution.py:146
  99.4 5.2 %fusion.22 = f32[512,704]{0,1:T(8,128)} fusion(bf16[512,2048]{1,0:T(8,128)(2,1)} %bitcast.21, bf16[1,1,2048,704]{2,3,1,0:T(8,128)(2,1)} %param.19), kind=kOutput, calls=%fused_computation.28 | convolution fusion | flops 1476395008 | bytes 6422528 | tf_op jit(solution)/shard_map/dot_general | solution.py:24
  104.6 7.7 %convolution_convert_fusion.4 = bf16[512,2048]{1,0:T(8,128)(2,1)} fusion(bf16[1,1,704,2048]{3,2,1,0:T(8,128)(2,1)S(1)} %copy-done, bf16[512,2048]{1,0:T(8,128)(2,1)} %bitcast.21, bf16[1,1,2048,704]{2,3,1,0:T(8,128)(2,1)} %param.20, f32[512,704]{0,1:T(8,128)} %fusion.22), kind=kOutput, calls=%fused_computation.13 | convolution fusion | flops 2956001280 | bytes 11403264 | tf_op jit(solution)/shard_map/dot_general | solution.py:27
  112.3 5.3 %all-to-all-start.1 = ((bf16[16,32,2048]{2,1,0:T(8,128)(2,1)}), bf16[16,32,2048]{2,1,0:T(8,128)(2,1)}, u32[]{:S(2)}, u32[]{:S(2)}) async-start(bf16[16,32,2048]{2,1,0:T(8,128)(2,1)} %bitcast.322), calls=%async_computation.1 | async-start | bytes 4194304 | tf_op jit(solution)/shard_map/all_to_all | solution.py:150
  117.6 1.3 rsqrt.32
  118.9 0.7 fusion.161
  119.6 1.5 fusion.109
  121.1 0.9 fusion.237
  122.0 60.0 %all-to-all-done.1 = bf16[16,32,2048]{2,1,0:T(8,128)(2,1)} async-done(((bf16[16,32,2048]{2,1,0:T(8,128)(2,1)}), bf16[16,32,2048]{2,1,0:T(8,128)(2,1)}, u32[]{:S(2)}, u32[]{:S(2)}) %all-to-all-start.1) | async-done | bytes 2097184 | tf_op jit(solution)/shard_map/all_to_all | solution.py:150
  182.0 2.9 fusion.143
  184.8 3.5 convolution_convert_fusion.8
  188.6 0.9 fusion.84
  189.6 3.4 fusion.48
  193.0 1.3 collective-permute-start
  194.3 8.5 %collective-permute-done = bf16[64,2048]{1,0:T(8,128)(2,1)} collective-permute-done((bf16[64,2048]{1,0:T(8,128)(2,1)S(1)}, bf16[64,2048]{1,0:T(8,128)(2,1)}, u32[]{:S(2)}, u32[]{:S(2)}) %collective-permute-start) | collective-permute-done | bytes 262176 | tf_op jit(solution)/shard_map/ppermute | solution.py:12
  202.7 1.1 fusion.104
  203.9 1.6 convolution_convert_fusion.3
  205.5 53.0 %all_to_all.30 = bf16[16,32,2048]{2,1,0:T(8,128)(2,1)S(1)} all-to-all(bf16[16,32,2048]{2,1,0:T(8,128)(2,1)S(1)} %bitcast.319), channel_id=1, replica_groups=mesh['section'=2,'expert'=16] {'expert'}, dimensions={0} | all-to-all | bytes 4194304 | tf_op jit(solution)/shard_map/all_to_all | solution.py:146
  258.5 1.4 copy-done.3
  259.9 2.8 fusion.20
  262.7 7.6 %convolution_convert_fusion.2 = bf16[512,2048]{1,0:T(8,128)(2,1)} fusion(bf16[1,1,704,2048]{3,2,1,0:T(8,128)(2,1)S(1)} %copy-done, bf16[512,2048]{1,0:T(8,128)(2,1)} %bitcast.324, bf16[1,1,2048,704]{2,3,1,0:T(8,128)(2,1)} %param.20, f32[512,704]{0,1:T(8,128)} %fusion.20), kind=kOutput, calls=%fused_computation.11 | convolution fusion | flops 2956001280 | bytes 11403264 | tf_op jit(solution)/shard_map/dot_general | solution.py:27
  270.4 5.0 %all-to-all-start.3 = ((bf16[16,32,2048]{2,1,0:T(8,128)(2,1)}), bf16[16,32,2048]{2,1,0:T(8,128)(2,1)}, u32[]{:S(2)}, u32[]{:S(2)}) async-start(bf16[16,32,2048]{2,1,0:T(8,128)(2,1)} %bitcast.321), calls=%async_computation.3 | async-start | bytes 4194304 | tf_op jit(solution)/shard_map/all_to_all | solution.py:150
  275.4 0.5 iota_compare_fusion.7
  275.9 0.7 fusion.163
  276.6 1.4 fusion.239
  278.0 3.6 convolution_convert_fusion.7
  281.5 0.7 copy-done.10
  282.2 0.6 fusion.240
  282.8 1.9 fusion.246
  284.7 2.7 fusion.85
  287.4 35.5 %all-to-all-done.3 = bf16[16,32,2048]{2,1,0:T(8,128)(2,1)} async-done(((bf16[16,32,2048]{2,1,0:T(8,128)(2,1)}), bf16[16,32,2048]{2,1,0:T(8,128)(2,1)}, u32[]{:S(2)}, u32[]{:S(2)}) %all-to-all-start.3) | async-done | bytes 2097184 | tf_op jit(solution)/shard_map/all_to_all | solution.py:150
  322.9 2.1 fusion.140
  325.0 3.8 fusion.45
  328.8 1.3 collective-permute-start.1
  330.1 8.7 %collective-permute-done.1 = bf16[64,2048]{1,0:T(8,128)(2,1)} collective-permute-done((bf16[64,2048]{1,0:T(8,128)(2,1)}, bf16[64,2048]{1,0:T(8,128)(2,1)}, u32[]{:S(2)}, u32[]{:S(2)}) %collective-permute-start.1) | collective-permute-done | bytes 262176 | tf_op jit(solution)/shard_map/ppermute | solution.py:12
  338.8 1.1 fusion.105
  339.9 1.6 convolution_convert_fusion.1
  341.6 53.0 %all_to_all.31 = bf16[16,32,2048]{2,1,0:T(8,128)(2,1)S(1)} all-to-all(bf16[16,32,2048]{2,1,0:T(8,128)(2,1)S(1)} %bitcast.318), channel_id=1, replica_groups=mesh['section'=2,'expert'=16] {'expert'}, dimensions={0} | all-to-all | bytes 4194304 | tf_op jit(solution)/shard_map/all_to_all | solution.py:146
  394.5 1.4 copy-done.4
  396.0 2.8 fusion.18
  398.8 7.6 %convolution_convert_fusion = bf16[512,2048]{1,0:T(8,128)(2,1)} fusion(bf16[1,1,704,2048]{3,2,1,0:T(8,128)(2,1)S(1)} %copy-done, bf16[512,2048]{1,0:T(8,128)(2,1)} %bitcast.326, bf16[1,1,2048,704]{2,3,1,0:T(8,128)(2,1)} %param.20, f32[512,704]{0,1:T(8,128)} %fusion.18), kind=kOutput, calls=%fused_computation.9 | convolution fusion | flops 2956001280 | bytes 11403264 | tf_op jit(solution)/shard_map/dot_general | solution.py:27
  406.4 5.2 %all-to-all-start.5 = ((bf16[16,32,2048]{2,1,0:T(8,128)(2,1)}), bf16[16,32,2048]{2,1,0:T(8,128)(2,1)}, u32[]{:S(2)}, u32[]{:S(2)}) async-start(bf16[16,32,2048]{2,1,0:T(8,128)(2,1)} %bitcast.320), calls=%async_computation.5 | async-start | bytes 4194304 | tf_op jit(solution)/shard_map/all_to_all | solution.py:150
  411.7 3.6 convolution_convert_fusion.6
  415.7 1.7 fusion.86
  417.4 41.7 %all-to-all-done.5 = bf16[16,32,2048]{2,1,0:T(8,128)(2,1)} async-done(((bf16[16,32,2048]{2,1,0:T(8,128)(2,1)}), bf16[16,32,2048]{2,1,0:T(8,128)(2,1)}, u32[]{:S(2)}, u32[]{:S(2)}) %all-to-all-start.5) | async-done | bytes 2097184 | tf_op jit(solution)/shard_map/all_to_all | solution.py:150
  459.1 2.1 fusion.137
  461.2 3.1 fusion.51
  464.3 2.0 fusion.107
  (68 shorter events, 1.5 us)
Async XLA Ops:
  6.5 98.1 %copy-start = (bf16[1,1,704,2048]{3,2,1,0:T(8,128)(2,1)S(1)}, bf16[1,1,704,2048]{3,2,1,0:T(8,128)(2,1)}, u32[]{:S(2)}) copy-start(bf16[1,1,704,2048]{3,2,1,0:T(8,128)(2,1)} %param.21) | copy-start | bytes 8650756
  6.5 13.2 %copy-start.1 = (bf16[4,32,2048]{2,1,0:T(8,128)(2,1)S(1)}, bf16[4,32,2048]{2,1,0:T(8,128)(2,1)}, u32[]{:S(2)}) copy-start(bf16[4,32,2048]{2,1,0:T(8,128)(2,1)} %param.12) | copy-start | bytes 1572868
  6.5 15.0 %copy-start.13 = (f32[1,2048]{1,0:T(1,128)S(1)}, f32[1,2048]{1,0:T(1,128)}, u32[]{:S(2)}) copy-start(f32[1,2048]{1,0:T(1,128)} %param.14) | copy-start | bytes 24580
  6.5 178.3 %all-gather.4.cloned.1.call-start = ((), (), s32[]{:S(2)}) async-start(), calls=%async_computation.6 | async-start | bytes 5570560 | tf_op jit(solution)/shard_map/all_gather | solution.py:72
  21.0 2.8 copy-start.8
  21.0 0.6 copy-start.18
  23.8 75.6 %all-to-all-start = ((bf16[16,32,2048]{2,1,0:T(8,128)(2,1)}), bf16[16,32,2048]{2,1,0:T(8,128)(2,1)}, u32[]{:S(2)}, u32[]{:S(2)}) async-start(bf16[16,32,2048]{2,1,0:T(8,128)(2,1)} %bitcast.317), calls=%async_computation | async-start | bytes 4194304 | tf_op jit(solution)/shard_map/all_to_all | solution.py:146
  30.3 159.3 %all-gather.6.cloned.1.call-start = ((), (), s32[]{:S(2)}) async-start(), calls=%async_computation.7 | async-start | bytes 4456448 | tf_op jit(solution)/shard_map/all_gather | solution.py:78
  112.3 7.3 %copy-start.14 = (f32[1,2048]{1,0:T(1,128)S(1)}, f32[1,2048]{1,0:T(1,128)}, u32[]{:S(2)}) copy-start(f32[1,2048]{1,0:T(1,128)} %param.13) | copy-start | bytes 24580
  112.3 69.6 %all-to-all-start.1 = ((bf16[16,32,2048]{2,1,0:T(8,128)(2,1)}), bf16[16,32,2048]{2,1,0:T(8,128)(2,1)}, u32[]{:S(2)}, u32[]{:S(2)}) async-start(bf16[16,32,2048]{2,1,0:T(8,128)(2,1)} %bitcast.322), calls=%async_computation.1 | async-start | bytes 4194304 | tf_op jit(solution)/shard_map/all_to_all | solution.py:150
  122.0 62.8 %copy-start.7 = (bf16[64,2048]{1,0:T(8,128)(2,1)S(1)}, bf16[64,2048]{1,0:T(8,128)(2,1)}, u32[]{:S(2)}) copy-start(bf16[64,2048]{1,0:T(8,128)(2,1)} %fusion.109) | copy-start | bytes 786436
  184.8 3.5 copy-start.17
  188.3 1.2 copy-start.9
  189.5 13.2 %copy-start.2 = (bf16[2,32,2048]{2,1,0:T(8,128)(2,1)S(1)}, bf16[2,32,2048]{2,1,0:T(8,128)(2,1)}, u32[]{:S(2)}) copy-start(bf16[2,32,2048]{2,1,0:T(8,128)(2,1)} %get-tuple-element.11) | copy-start | bytes 786436
  192.9 9.8 %copy-start.5 = (bf16[64,2048]{1,0:T(8,128)(2,1)}, bf16[64,2048]{1,0:T(8,128)(2,1)S(1)}, u32[]{:S(2)}) copy-start(bf16[64,2048]{1,0:T(8,128)(2,1)S(1)} %fusion.48) | copy-start | bytes 786436
  193.0 9.8 %collective-permute-start = (bf16[64,2048]{1,0:T(8,128)(2,1)S(1)}, bf16[64,2048]{1,0:T(8,128)(2,1)}, u32[]{:S(2)}, u32[]{:S(2)}) collective-permute-start(bf16[64,2048]{1,0:T(8,128)(2,1)S(1)} %fusion.48), channel_id=1, source_target_pairs={{0,16},{1,17},{2,18},{3,19},{4,20},{5,21},{6,22},{7,23},{8,24},{9,... | collective-permute-start | bytes 786440 | tf_op jit(solution)/shard_map/ppermute | solution.py:12
  203.9 1.6 copy-start.19
  205.5 54.4 %copy-start.21 = (bf16[1,1,2048,704]{2,3,1,0:T(8,128)(2,1)S(1)}, bf16[1,1,2048,704]{2,3,1,0:T(8,128)(2,1)}, u32[]{:S(2)}) copy-start(bf16[1,1,2048,704]{2,3,1,0:T(8,128)(2,1)} %param.19) | copy-start | bytes 8650756
  258.5 1.4 copy-start.3
  270.4 52.5 %all-to-all-start.3 = ((bf16[16,32,2048]{2,1,0:T(8,128)(2,1)}), bf16[16,32,2048]{2,1,0:T(8,128)(2,1)}, u32[]{:S(2)}, u32[]{:S(2)}) async-start(bf16[16,32,2048]{2,1,0:T(8,128)(2,1)} %bitcast.321), calls=%async_computation.3 | async-start | bytes 4194304 | tf_op jit(solution)/shard_map/all_to_all | solution.py:150
  281.5 0.7 copy-start.10
  322.9 2.1 copy-start.12
  328.8 9.9 %collective-permute-start.1 = (bf16[64,2048]{1,0:T(8,128)(2,1)}, bf16[64,2048]{1,0:T(8,128)(2,1)}, u32[]{:S(2)}, u32[]{:S(2)}) collective-permute-start(bf16[64,2048]{1,0:T(8,128)(2,1)} %fusion.45), channel_id=1, source_target_pairs={{0,16},{1,17},{2,18},{3,19},{4,20},{5,21},{6,22},{7,23},{8,24},{9,... | collective-permute-start | bytes 786440 | tf_op jit(solution)/shard_map/ppermute | solution.py:12
  341.6 54.4 %copy-start.22 = (bf16[1,1,2048,704]{2,3,1,0:T(8,128)(2,1)S(1)}, bf16[1,1,2048,704]{2,3,1,0:T(8,128)(2,1)}, u32[]{:S(2)}) copy-start(bf16[1,1,2048,704]{2,3,1,0:T(8,128)(2,1)} %param.19) | copy-start | bytes 8650756
  394.5 1.4 copy-start.4
  406.4 5.2 %copy-start.20 = (pred[128]{0:T(512)(128)(4,1)S(1)}, pred[128]{0:T(512)(128)(4,1)}, u32[]{:S(2)}) copy-start(pred[128]{0:T(512)(128)(4,1)} %get-tuple-element.22) | copy-start | bytes 388
  406.4 52.7 %all-to-all-start.5 = ((bf16[16,32,2048]{2,1,0:T(8,128)(2,1)}), bf16[16,32,2048]{2,1,0:T(8,128)(2,1)}, u32[]{:S(2)}, u32[]{:S(2)}) async-start(bf16[16,32,2048]{2,1,0:T(8,128)(2,1)} %bitcast.320), calls=%async_computation.5 | async-start | bytes 4194304 | tf_op jit(solution)/shard_map/all_to_all | solution.py:150
  411.7 3.6 copy-start.16
  411.7 4.0 copy-start.15
  417.3 43.8 %copy-start.11 = (bf16[8,8,8,128]{3,2,1,0:T(8,128)(2,1)S(1)}, bf16[8,8,8,128]{3,2,1,0:T(8,128)(2,1)}, u32[]{:S(2)}) copy-start(bf16[8,8,8,128]{3,2,1,0:T(8,128)(2,1)} %fusion.86) | copy-start | bytes 393220
  461.2 3.1 copy-start.6
Sparse Core Ops, SparseCore 0:
  9.6 78.9 all-gather.3
  90.8 78.2 all-gather.5
where the time goes:
time: 475 us; the launch traced here: 473 us
  waiting for transfers between devices  223 us (47%)
  blocking collectives  106 us (22%)
  matrix products  74.9 us (16%)
  starting transfers between devices  24.6 us (5%)
  other arithmetic  18.6 us (4%)
  between operations  13.8 us (3%)
  local copies, waits for them, and re-layouts  12 us (3%)
    all_to_all x3, waiting for transfers between devices, mixture(): lax.all_to_all(produced, 'expert', split_axis=0, concat_axis=0, tiled=True)  137 us
    all_to_all x2, blocking collectives, mixture(): lax.all_to_all(outgoing, 'expert', split_axis=0, concat_axis=0, tiled=True)  106 us
    all_to_all x1, waiting for transfers between devices, mixture(): lax.all_to_all(outgoing, 'expert', split_axis=0, concat_axis=0, tiled=True)  68.3 us
    dot_general x3, matrix products, expert_rows(): jnp.dot(hidden, down_matrix, preferred_element_type=jnp.float32)  23 us
    ppermute x2, waiting for transfers between devices, shifted(): lax.ppermute(value, axis, [(source, source + steps) for source in range(i...  17.1 us
    all_to_all x3, starting transfers between devices, mixture(): lax.all_to_all(produced, 'expert', split_axis=0, concat_axis=0, tiled=True)  15.5 us
    dot_general x3, matrix products, expert_rows(): gated = jnp.dot(slot_rows, gate_matrix, preferred_element_type=jnp.float32)  10.8 us
    dot_general x3, matrix products, attend(): jnp.dot(normed, full_mixed, preferred_element_type=jnp.float32)  10.6 us
  transfers between devices with their start and end apart: 8, of which 6 were waited for; matrix products, arithmetic and copies ran while one was open for 12% of the time, Pallas kernels for 0%

commit v1 on v0

--- a/solution.py
+++ b/solution.py
@@ -1,6 +1,10 @@
+import functools
+
 import jax
 import jax.numpy as jnp
 from jax import lax
+from jax.experimental import pallas as pl
+from jax.experimental.pallas import tpu as pltpu
 from jax.sharding import PartitionSpec as P
 
 epsilon = 1e-06
@@ -40,10 +44,120 @@
         columns[:, None] == jnp.arange(expert_count * capacity, dtype=jnp.int32)[None, :]
     ).astype(jnp.float32)
     onehot = onehot.reshape(tok_rows, pick_count, expert_count * capacity)
-    scatter_table = jnp.sum(onehot, axis=1).astype(jnp.bfloat16)
+    named_slots = jnp.sum(
+        (matches * (slot_ranks + 1)[:, None]).reshape(tok_rows, pick_count, expert_count), axis=1
+    ).astype(jnp.bfloat16)
+    named_slots = jnp.pad(named_slots, ((0, 0), (0, -expert_count % 128)))
     pick_weights = codes_block.astype(jnp.float32) / 64.0
     combine_table = jnp.sum(onehot * pick_weights[:, :, None], axis=1).astype(jnp.bfloat16)
-    return (scatter_table, combine_table)
+    return (named_slots, combine_table)
+
+
+def gather_kernel(device_count, operand_count, *refs):
+    sources, targets = refs[:operand_count], refs[operand_count : 2 * operand_count]
+    own_sem, send_z, recv_z, send_y, recv_y, send_c, recv_c = refs[2 * operand_count :]
+    me = lax.axis_index("expert")
+    depth = device_count // 4
+    place_c, place_y, place_z = lax.rem(me, 2), lax.rem(me // 2, 2), me // 4
+
+    def index_of(z, y, c):
+        return (z * 2 + y) * 2 + c
+
+    partners = [index_of(lax.rem(place_z + k, depth), place_y, place_c) for k in range(1, depth)]
+    origins = [
+        index_of(lax.rem(place_z + depth - k, depth), place_y, place_c) for k in range(depth)
+    ]
+    crossed = [
+        index_of(lax.rem(place_z + depth - k, depth), 1 - place_y, place_c) for k in range(depth)
+    ]
+    partner_y = index_of(place_z, 1 - place_y, place_c)
+    partner_c = index_of(place_z, place_y, 1 - place_c)
+
+    barrier = pltpu.get_barrier_semaphore()
+    for peer in partners + [partner_y, partner_c]:
+        pl.semaphore_signal(
+            barrier, inc=1, device_id={"expert": peer}, device_id_type=pl.DeviceIdType.MESH
+        )
+    pl.semaphore_wait(barrier, depth + 1)
+
+    def send(source, target, send_sem, recv_sem, peer):
+        copy = pltpu.make_async_remote_copy(
+            src_ref=source,
+            dst_ref=target,
+            send_sem=send_sem,
+            recv_sem=recv_sem,
+            device_id={"expert": peer},
+            device_id_type=pl.DeviceIdType.MESH,
+        )
+        copy.start()
+        return copy
+
+    owned = []
+    along_z = [[None] * depth for _ in range(operand_count)]
+    along_y = [[None] * depth for _ in range(operand_count)]
+    along_c = [[None] * (2 * depth) for _ in range(operand_count)]
+    for a in range(operand_count):
+        for k in range(1, depth):
+            along_z[a][k] = send(
+                sources[a],
+                targets[a].at[me],
+                send_z.at[a, k],
+                recv_z.at[a, k],
+                partners[k - 1],
+            )
+        along_y[a][0] = send(
+            sources[a], targets[a].at[me], send_y.at[a, 0], recv_y.at[a, 0], partner_y
+        )
+        along_c[a][0] = send(
+            sources[a], targets[a].at[me], send_c.at[a, 0], recv_c.at[a, 0], partner_c
+        )
+        owned.append(pltpu.make_async_copy(sources[a], targets[a].at[me], own_sem.at[a]))
+        owned[a].start()
+    for a in range(operand_count):
+        for k in range(1, depth):
+            along_z[a][k].wait_recv()
+            block = targets[a].at[origins[k]]
+            along_y[a][k] = send(block, block, send_y.at[a, k], recv_y.at[a, k], partner_y)
+            along_c[a][k] = send(block, block, send_c.at[a, k], recv_c.at[a, k], partner_c)
+    for a in range(operand_count):
+        for k in range(depth):
+            along_y[a][k].wait_recv()
+            block = targets[a].at[crossed[k]]
+            along_c[a][depth + k] = send(
+                block, block, send_c.at[a, depth + k], recv_c.at[a, depth + k], partner_c
+            )
+    for a in range(operand_count):
+        for k in range(2 * depth):
+            along_c[a][k].wait_recv()
+        for copy in along_z[a][1:] + along_y[a] + along_c[a]:
+            copy.wait_send()
+        owned[a].wait()
+
+
+def gather_all(operands, collective_id):
+    device_count, operand_count = lax.axis_size("expert"), len(operands)
+    depth = device_count // 4
+    pairs = pltpu.SemaphoreType.DMA((operand_count, depth))
+    doubles = pltpu.SemaphoreType.DMA((operand_count, 2 * depth))
+    return pl.pallas_call(
+        functools.partial(gather_kernel, device_count, operand_count),
+        out_shape=[
+            jax.ShapeDtypeStruct((device_count,) + operand.shape, operand.dtype)
+            for operand in operands
+        ],
+        in_specs=[pl.BlockSpec(memory_space=pltpu.VMEM)] * operand_count,
+        out_specs=[pl.BlockSpec(memory_space=pl.ANY)] * operand_count,
+        scratch_shapes=[
+            pltpu.SemaphoreType.DMA((operand_count,)),
+            pairs,
+            pairs,
+            pairs,
+            pairs,
+            doubles,
+            doubles,
+        ],
+        compiler_params=pltpu.CompilerParams(collective_id=collective_id, has_side_effects=True),
+    )(*operands)
 
 
 def shards(
@@ -69,13 +183,15 @@
     capacity = min(tok_rows, tok_rows * pick_count * 4 // (3 * expert_count))
     head_size = key_weight.shape[-1]
     head_count = query_weight.shape[-1] // head_size
-    full_mixed = lax.all_gather(
-        jnp.concatenate([query_weight[0], key_weight[0], value_weight[0]], axis=-1),
-        "expert",
-        axis=0,
-        tiled=True,
-    )
-    full_out = lax.all_gather(out_weight[0], "expert", axis=0, tiled=True)
+    mixed_blocks, out_blocks = gather_all(
+        [
+            jnp.concatenate([query_weight[0], key_weight[0], value_weight[0]], axis=-1),
+            out_weight[0],
+        ],
+        0,
+    )
+    full_mixed = mixed_blocks.reshape(model_width, -1)
+    full_out = out_blocks.reshape(-1, model_width)
     members = 2 if section_count <= 2 and micro_count % 2 == 0 else 1
     group_count, block_rows = micro_count // members, members * tok_rows
     lag = 1
@@ -90,10 +206,10 @@
     def member_tables(picks, codes, member):
         return route_tables(picks, codes, expert_count, capacity, member, members)
 
-    scatter_tables, combine_tables = jax.vmap(member_tables)(
+    slot_tables, combine_tables = jax.vmap(member_tables)(
         routes[0], weights_code[0], jnp.arange(micro_count, dtype=jnp.int32) % members
     )
-    scatter_tables = scatter_tables.reshape(group_count, block_rows, -1)
+    slot_tables = slot_tables.reshape(group_count, block_rows, -1)
     combine_tables = combine_tables.reshape(group_count, block_rows, -1)
     token_groups = tokens.reshape(group_count, block_rows, model_width)
 
@@ -137,13 +253,21 @@
         )
         return jnp.dot(attended_values, full_out, preferred_element_type=jnp.float32)
 
-    def mixture(wide_input, scatter_table, combine_table):
+    def mixture(wide_input, slot_table, combine_table):
         moe_input = rms_scale(wide_input, moe_gain).astype(jnp.bfloat16)
-        outgoing = jnp.einsum(
-            "te,td->ed", scatter_table, moe_input, preferred_element_type=jnp.float32
-        )
-        outgoing = outgoing.astype(jnp.bfloat16).reshape(expert_count, group_slots, model_width)
-        arrived = lax.all_to_all(outgoing, "expert", split_axis=0, concat_axis=0, tiled=True)
+        (gathered,) = gather_all([jnp.concatenate([moe_input, slot_table], axis=-1)], 1)
+        named = lax.dynamic_slice_in_dim(
+            gathered, model_width + lax.axis_index("expert"), 1, axis=2
+        ).reshape(expert_devices, members, 1, tok_rows)
+        slots = jnp.arange(1, capacity + 1, dtype=jnp.int32).astype(jnp.bfloat16)
+        chosen = (named == slots[None, None, :, None]).astype(jnp.bfloat16)
+        source_rows = gathered[:, :, :model_width].reshape(
+            expert_devices, members, tok_rows, model_width
+        )
+        arrived = jnp.einsum(
+            "nmsi,nmid->nmsd", chosen, source_rows, preferred_element_type=jnp.float32
+        )
+        arrived = arrived.astype(jnp.bfloat16).reshape(expert_count, group_slots, model_width)
         produced = expert_rows(
             arrived.reshape(-1, model_width), gate_matrix, up_matrix, down_matrix
         ).reshape(arrived.shape)
@@ -161,7 +285,7 @@
         wide_input = layer_input.astype(jnp.float32)
         mixed = mixture(
             wide_input,
-            lax.dynamic_index_in_dim(scatter_tables, clipped, 0, keepdims=False),
+            lax.dynamic_index_in_dim(slot_tables, clipped, 0, keepdims=False),
             lax.dynamic_index_in_dim(combine_tables, clipped, 0, keepdims=False),
         )
         attended = attend(wide_input, tick, keys, values)

time: 475 us -> 489 us (1.029)
  Pallas kernels: 0 us -> 231 us
  waiting for transfers between devices: 223 us -> 94.3 us
  blocking collectives: 106 us -> 0 us
  local copies, waits for them, and re-layouts: 12 us -> 31.3 us
  between operations: 13.8 us -> 0.52 us
  starting transfers between devices: 24.6 us -> 36 us
    pallas_call x0 -> x4, Pallas kernels: none -> 231 us  [gather_all(): pl.pallas_call(functools.partial(gather_kernel, device_count, operand_cou...]
    all_to_all x2 -> x0, blocking collectives: 106 us -> none  [mixture(): lax.all_to_all(outgoing, 'expert', split_axis=0, concat_axis=0, tiled=True)]
    all_to_all x1 -> x0, waiting for transfers between devices: 68.3 us -> none  [mixture(): lax.all_to_all(outgoing, 'expert', split_axis=0, concat_axis=0, tiled=True)]
    all_to_all x3, waiting for transfers between devices: 137 us -> 77.9 us  [mixture(): lax.all_to_all(produced, 'expert', split_axis=0, concat_axis=0, tiled=True)]
    all_to_all x3, starting transfers between devices: 15.5 us -> 33 us  [mixture(): lax.all_to_all(produced, 'expert', split_axis=0, concat_axis=0, tiled=True)]
    slice x2 -> x5, local copies, waits for them, and re-layouts: 1.67 us -> 14.4 us  [the longest x3 14.2 us: mixture(): gathered[:, :, :model_width]]
    all_to_all x1 -> x0, starting transfers between devices: 6.51 us -> none  [mixture(): lax.all_to_all(outgoing, 'expert', split_axis=0, concat_axis=0, tiled=True)]
  transfers between devices with their start and end apart: 8 -> 5, of which waited for: 6 -> 4; matrix products, arithmetic and copies ran while one was open for 12% -> 7% of each run, Pallas kernels for 0% -> 23%
where the time goes in v1:
time: 489 us; the launch traced here: 487 us
  Pallas kernels  231 us (47%)
  waiting for transfers between devices  94.3 us (19%)
  matrix products  78.1 us (16%)
  starting transfers between devices  36 us (7%)
  local copies, waits for them, and re-layouts  31.3 us (6%)
  other arithmetic  16.1 us (3%)
    pallas_call x4, Pallas kernels, gather_all(): pl.pallas_call(functools.partial(gather_kernel, device_count, operand_cou...  231 us
    all_to_all x3, waiting for transfers between devices, mixture(): lax.all_to_all(produced, 'expert', split_axis=0, concat_axis=0, tiled=True)  77.9 us
    all_to_all x3, starting transfers between devices, mixture(): lax.all_to_all(produced, 'expert', split_axis=0, concat_axis=0, tiled=True)  33 us
    dot_general x3, matrix products, expert_rows(): jnp.dot(hidden, down_matrix, preferred_element_type=jnp.float32)  23 us
    ppermute x2, waiting for transfers between devices, shifted(): lax.ppermute(value, axis, [(source, source + steps) for source in range(i...  16.4 us
    slice x3, local copies, waits for them, and re-layouts, mixture(): gathered[:, :, :model_width]  14.2 us
    dot_general x3, matrix products, attend(): jnp.dot(normed, full_mixed, preferred_element_type=jnp.float32)  11.3 us
    dot_general x3, matrix products, attend(): jnp.dot(attended_values, full_out, preferred_element_type=jnp.float32)  10 us
  transfers between devices with their start and end apart: 5, of which 4 were waited for; matrix products, arithmetic and copies ran while one was open for 7% of the time, Pallas kernels for 23%

profile of v1, /device:TPU:15, one launch (start us, length us, event | category | flops | bytes accessed | tf_op | source)
XLA Modules:
  0.0 487.3 jit_solution(4200503366148595514)
XLA Ops:
  0.0 1.0 copy.57
  1.0 0.7 copy.136
  1.8 2.3 reduce-window.6
  4.9 1.1 multiply_reduce_fusion
  6.1 1.1 fusion.79
  7.8 0.7 pad_maximum_fusion.1.refs_0_
  8.6 37.6 %shard_map.119 = bf16[16,64,2176]{2,1,0:T(8,128)(2,1)} custom-call(bf16[64,2176]{1,0:T(8,128)(2,1)} %pad_maximum_fusion.1.refs_0_), custom_call_target="tpu_custom_call" | custom-call | tf_op jit(solution)/shard_map/pallas_call | solution.py:142
  46.2 4.7 slice.61
  50.9 1.3 dynamic-slice_reduce_fusion.2
  52.3 3.1 convolution_convert_fusion.5
  55.4 1.3 copy-done.4
  56.8 2.8 fusion.16
  59.6 7.7 %convolution_convert_fusion.4 = bf16[512,2048]{1,0:T(8,128)(2,1)} fusion(bf16[1,1,704,2048]{3,2,1,0:T(8,128)(2,1)S(1)} %copy-done, bf16[512,2048]{1,0:T(8,128)(2,1)} %bitcast.315, bf16[1,1,2048,704]{2,3,1,0:T(8,128)(2,1)} %param.20, f32[512,704]{0,1:T(8,128)} %fusion.16), kind=kOutput, calls=%fused_computation.7 | convolution fusion | flops 2956001280 | bytes 11403264 | tf_op jit(solution)/shard_map/dot_general | solution.py:31
  67.3 11.8 %all-to-all-start = ((bf16[16,32,2048]{2,1,0:T(8,128)(2,1)}), bf16[16,32,2048]{2,1,0:T(8,128)(2,1)}, u32[]{:S(2)}, u32[]{:S(2)}) async-start(bf16[16,32,2048]{2,1,0:T(8,128)(2,1)} %bitcast.309), calls=%async_computation | async-start | bytes 4194304 | tf_op jit(solution)/shard_map/all_to_all | solution.py:274
  79.0 0.7 copy.63
  79.7 0.7 multiply_bitcast_fusion
  81.0 1.7 pad_maximum_fusion.refs_0_
  82.7 110.9 %shard_map.118 = (bf16[16,128,1280]{2,1,0:T(8,128)(2,1)}, bf16[16,64,2048]{2,1,0:T(8,128)(2,1)}) custom-call(bf16[128,1280]{1,0:T(8,128)(2,1)} %pad_maximum_fusion.refs_0_, bf16[64,2048]{1,0:T(8,128)(2,1)} %bitcast.326), custom_call_target="tpu_custom_call" | custom-call | tf_op jit(solution)/shard_map/pallas_call | solution.py:142
  193.9 4.2 convolution_convert_fusion.8
  198.1 1.9 fusion.205
  200.0 1.2 fusion.54
  201.2 1.0 select_reduce_fusion
  202.2 0.8 fusion.201
  203.0 3.9 convolution_add_fusion.3
  206.9 2.2 fusion.20
  209.1 1.5 collective-permute-start
  210.6 8.3 %collective-permute-done = bf16[64,2048]{1,0:T(8,128)(2,1)} collective-permute-done((bf16[64,2048]{1,0:T(8,128)(2,1)S(1)}, bf16[64,2048]{1,0:T(8,128)(2,1)}, u32[]{:S(2)}, u32[]{:S(2)}) %collective-permute-start) | collective-permute-done | bytes 262176 | tf_op jit(solution)/shard_map/ppermute | solution.py:16
  218.8 1.1 fusion.74
  220.7 1.4 pad_maximum_fusion.2.refs_0_
  222.2 44.8 %shard_map.120 = bf16[16,64,2176]{2,1,0:T(8,128)(2,1)} custom-call(bf16[64,2176]{1,0:T(8,128)(2,1)} %pad_maximum_fusion.2.refs_0_), custom_call_target="tpu_custom_call" | custom-call | tf_op jit(solution)/shard_map/pallas_call | solution.py:142
  267.0 4.7 slice.66
  271.7 1.9 dynamic-slice_reduce_fusion.1
  273.6 1.3 eq.153
  274.9 3.1 convolution_convert_fusion.3
  278.0 1.4 copy-done.5
  279.4 2.8 fusion.14
  282.2 7.7 %convolution_convert_fusion.2 = bf16[512,2048]{1,0:T(8,128)(2,1)} fusion(bf16[1,1,704,2048]{3,2,1,0:T(8,128)(2,1)S(1)} %copy-done, bf16[512,2048]{1,0:T(8,128)(2,1)} %bitcast.317, bf16[1,1,2048,704]{2,3,1,0:T(8,128)(2,1)} %param.20, f32[512,704]{0,1:T(8,128)} %fusion.14), kind=kOutput, calls=%fused_computation.5 | convolution fusion | flops 2956001280 | bytes 11403264 | tf_op jit(solution)/shard_map/dot_general | solution.py:31
  289.9 11.0 %all-to-all-start.1 = ((bf16[16,32,2048]{2,1,0:T(8,128)(2,1)}), bf16[16,32,2048]{2,1,0:T(8,128)(2,1)}, u32[]{:S(2)}, u32[]{:S(2)}) async-start(bf16[16,32,2048]{2,1,0:T(8,128)(2,1)} %bitcast.311), calls=%async_computation.1 | async-start | bytes 4194304 | tf_op jit(solution)/shard_map/all_to_all | solution.py:274
  301.4 0.7 fusion.130
  302.1 3.6 convolution_convert_fusion.7
  305.6 0.7 copy-done.10
  306.3 1.4 fusion.203
  307.7 1.9 fusion.210
  309.6 2.6 fusion.55
  312.2 36.2 %all-to-all-done.1 = bf16[16,32,2048]{2,1,0:T(8,128)(2,1)} async-done(((bf16[16,32,2048]{2,1,0:T(8,128)(2,1)}), bf16[16,32,2048]{2,1,0:T(8,128)(2,1)}, u32[]{:S(2)}, u32[]{:S(2)}) %all-to-all-start.1) | async-done | bytes 2097184 | tf_op jit(solution)/shard_map/all_to_all | solution.py:274
  348.4 2.1 fusion.105
  350.6 3.1 fusion.21
  353.7 1.5 collective-permute-start.1
  355.2 8.1 %collective-permute-done.1 = bf16[64,2048]{1,0:T(8,128)(2,1)S(1)} collective-permute-done((bf16[64,2048]{1,0:T(8,128)(2,1)S(1)}, bf16[64,2048]{1,0:T(8,128)(2,1)S(1)}, u32[]{:S(2)}, u32[]{:S(2)}) %collective-permute-start.1) | collective-permute-done | bytes 262176 | tf_op jit(solution)/shard_map/ppermute | solution.py:16
  363.7 0.7 pad_maximum_fusion.3.refs_0_
  364.4 37.7 %shard_map.121 = bf16[16,64,2176]{2,1,0:T(8,128)(2,1)} custom-call(bf16[64,2176]{1,0:T(8,128)(2,1)} %pad_maximum_fusion.3.refs_0_), custom_call_target="tpu_custom_call" | custom-call | tf_op jit(solution)/shard_map/pallas_call | solution.py:142
  402.2 4.7 slice.70
  406.9 1.3 dynamic-slice_reduce_fusion
  408.3 3.1 convolution_convert_fusion.1
  411.4 1.4 copy-done.3
  412.8 2.8 fusion.12
  415.6 7.7 %convolution_convert_fusion = bf16[512,2048]{1,0:T(8,128)(2,1)} fusion(bf16[1,1,704,2048]{3,2,1,0:T(8,128)(2,1)S(1)} %copy-done, bf16[512,2048]{1,0:T(8,128)(2,1)} %bitcast.313, bf16[1,1,2048,704]{2,3,1,0:T(8,128)(2,1)} %param.20, f32[512,704]{0,1:T(8,128)} %fusion.12), kind=kOutput, calls=%fused_computation.3 | convolution fusion | flops 2956001280 | bytes 11403264 | tf_op jit(solution)/shard_map/dot_general | solution.py:31
  423.3 10.2 %all-to-all-start.2 = ((bf16[16,32,2048]{2,1,0:T(8,128)(2,1)}), bf16[16,32,2048]{2,1,0:T(8,128)(2,1)}, u32[]{:S(2)}, u32[]{:S(2)}) async-start(bf16[16,32,2048]{2,1,0:T(8,128)(2,1)} %bitcast.310), calls=%async_computation.2 | async-start | bytes 4194304 | tf_op jit(solution)/shard_map/all_to_all | solution.py:274
  433.6 3.6 convolution_convert_fusion.6
  437.6 1.7 fusion.56
  439.3 41.7 %all-to-all-done.2 = bf16[16,32,2048]{2,1,0:T(8,128)(2,1)} async-done(((bf16[16,32,2048]{2,1,0:T(8,128)(2,1)}), bf16[16,32,2048]{2,1,0:T(8,128)(2,1)}, u32[]{:S(2)}, u32[]{:S(2)}) %all-to-all-start.2) | async-done | bytes 2097184 | tf_op jit(solution)/shard_map/all_to_all | solution.py:274
  481.0 2.1 fusion.103
  483.1 3.1 fusion.23
  486.2 1.1 fusion.77
  (91 shorter events, 4.8 us)
Async XLA Ops:
  0.0 59.6 %copy-start = (bf16[1,1,704,2048]{3,2,1,0:T(8,128)(2,1)S(1)}, bf16[1,1,704,2048]{3,2,1,0:T(8,128)(2,1)}, u32[]{:S(2)}) copy-start(bf16[1,1,704,2048]{3,2,1,0:T(8,128)(2,1)} %param.21) | copy-start | bytes 8650756
  1.7 50.6 %copy-start.20 = (bf16[16]{0:T(256)(128)(2,1)}, bf16[16]{0:T(256)(128)(2,1)S(1)}, u32[]{:S(2)}) copy-start(bf16[16]{0:T(256)(128)(2,1)S(1)} %add_convert_fusion) | copy-start | bytes 100
  52.3 4.5 copy-start.24
  55.4 1.4 copy-start.4
  67.2 13.8 %copy-start.16 = (bf16[1,128,128]{2,1,0:T(8,128)(2,1)S(1)}, bf16[1,128,128]{2,1,0:T(8,128)(2,1)}, u32[]{:S(2)}) copy-start(bf16[1,128,128]{2,1,0:T(8,128)(2,1)} %param.17) | copy-start | bytes 98308
  67.2 13.8 %copy-start.17 = (bf16[1,128,128]{2,1,0:T(8,128)(2,1)S(1)}, bf16[1,128,128]{2,1,0:T(8,128)(2,1)}, u32[]{:S(2)}) copy-start(bf16[1,128,128]{2,1,0:T(8,128)(2,1)} %param.16) | copy-start | bytes 98308
  67.3 126.5 %copy-start.1 = (bf16[4,32,2048]{2,1,0:T(8,128)(2,1)S(1)}, bf16[4,32,2048]{2,1,0:T(8,128)(2,1)}, u32[]{:S(2)}) copy-start(bf16[4,32,2048]{2,1,0:T(8,128)(2,1)} %param.12) | copy-start | bytes 1572868
  67.3 126.5 %copy-start.14 = (f32[1,2048]{1,0:T(1,128)S(1)}, f32[1,2048]{1,0:T(1,128)}, u32[]{:S(2)}) copy-start(f32[1,2048]{1,0:T(1,128)} %param.13) | copy-start | bytes 24580
  67.3 139.6 %all-to-all-start = ((bf16[16,32,2048]{2,1,0:T(8,128)(2,1)}), bf16[16,32,2048]{2,1,0:T(8,128)(2,1)}, u32[]{:S(2)}, u32[]{:S(2)}) async-start(bf16[16,32,2048]{2,1,0:T(8,128)(2,1)} %bitcast.309), calls=%async_computation | async-start | bytes 4194304 | tf_op jit(solution)/shard_map/all_to_all | solution.py:274
  206.8 12.0 %copy-start.2 = (bf16[2,32,2048]{2,1,0:T(8,128)(2,1)S(1)}, bf16[2,32,2048]{2,1,0:T(8,128)(2,1)}, u32[]{:S(2)}) copy-start(bf16[2,32,2048]{2,1,0:T(8,128)(2,1)} %get-tuple-element.13) | copy-start | bytes 786436
  206.8 13.7 %copy-start.13 = (f32[1,2048]{1,0:T(1,128)S(1)}, f32[1,2048]{1,0:T(1,128)}, u32[]{:S(2)}) copy-start(f32[1,2048]{1,0:T(1,128)} %param.14) | copy-start | bytes 24580
  209.1 9.8 %copy-start.6 = (bf16[64,2048]{1,0:T(8,128)(2,1)}, bf16[64,2048]{1,0:T(8,128)(2,1)S(1)}, u32[]{:S(2)}) copy-start(bf16[64,2048]{1,0:T(8,128)(2,1)S(1)} %fusion.20) | copy-start | bytes 786436
  209.1 9.8 %collective-permute-start = (bf16[64,2048]{1,0:T(8,128)(2,1)S(1)}, bf16[64,2048]{1,0:T(8,128)(2,1)}, u32[]{:S(2)}, u32[]{:S(2)}) collective-permute-start(bf16[64,2048]{1,0:T(8,128)(2,1)S(1)} %fusion.20), channel_id=1, source_target_pairs={{0,16},{1,17},{2,18},{3,19},{4,20},{5,21},{6,22},{7,23},{8,24},{9,... | collective-permute-start | bytes 786440 | tf_op jit(solution)/shard_map/ppermute | solution.py:16
  220.0 0.6 copy-start.22
  274.9 4.5 copy-start.25
  278.0 1.4 copy-start.5
  289.9 58.5 %all-to-all-start.1 = ((bf16[16,32,2048]{2,1,0:T(8,128)(2,1)}), bf16[16,32,2048]{2,1,0:T(8,128)(2,1)}, u32[]{:S(2)}, u32[]{:S(2)}) async-start(bf16[16,32,2048]{2,1,0:T(8,128)(2,1)} %bitcast.311), calls=%async_computation.1 | async-start | bytes 4194304 | tf_op jit(solution)/shard_map/all_to_all | solution.py:274
  305.6 0.7 copy-start.10
  348.4 2.1 copy-start.12
  350.6 13.1 %copy-start.15 = (bf16[64,128]{1,0:T(8,128)(2,1)S(1)}, bf16[64,128]{1,0:T(8,128)(2,1)}, u32[]{:S(2)}) copy-start(bf16[64,128]{1,0:T(8,128)(2,1)} %get-tuple-element.23) | copy-start | bytes 49156
  353.6 9.9 %copy-start.8 = (bf16[64,2048]{1,0:T(8,128)(2,1)}, bf16[64,2048]{1,0:T(8,128)(2,1)S(1)}, u32[]{:S(2)}) copy-start(bf16[64,2048]{1,0:T(8,128)(2,1)S(1)} %fusion.21) | copy-start | bytes 786436
  353.7 9.6 %collective-permute-start.1 = (bf16[64,2048]{1,0:T(8,128)(2,1)S(1)}, bf16[64,2048]{1,0:T(8,128)(2,1)S(1)}, u32[]{:S(2)}, u32[]{:S(2)}) collective-permute-start(bf16[64,2048]{1,0:T(8,128)(2,1)S(1)} %fusion.21), channel_id=1, source_target_pairs={{0,16},{1,17},{2,18},{3,19},{4,20},{5,21},{6,22},{7,23},{8,24},{9,... | collective-permute-start | bytes 786440 | tf_op jit(solution)/shard_map/ppermute | solution.py:16
  402.2 6.1 %copy-start.21 = (bf16[16]{0:T(256)(128)(2,1)S(1)}, bf16[16]{0:T(256)(128)(2,1)}, u32[]{:S(2)}) copy-start(bf16[16]{0:T(256)(128)(2,1)} %copy-done.20) | copy-start | bytes 100
  408.3 4.5 copy-start.26
  411.4 1.4 copy-start.3
  423.2 10.2 %copy-start.23 = (pred[128]{0:T(512)(128)(4,1)S(1)}, pred[128]{0:T(512)(128)(4,1)}, u32[]{:S(2)}) copy-start(pred[128]{0:T(512)(128)(4,1)} %get-tuple-element.29) | copy-start | bytes 388
  423.3 57.7 %all-to-all-start.2 = ((bf16[16,32,2048]{2,1,0:T(8,128)(2,1)}), bf16[16,32,2048]{2,1,0:T(8,128)(2,1)}, u32[]{:S(2)}, u32[]{:S(2)}) async-start(bf16[16,32,2048]{2,1,0:T(8,128)(2,1)} %bitcast.310), calls=%async_computation.2 | async-start | bytes 4194304 | tf_op jit(solution)/shard_map/all_to_all | solution.py:274
  433.6 3.6 copy-start.18
  433.6 4.0 copy-start.19
  439.3 43.8 %copy-start.11 = (bf16[8,8,8,128]{3,2,1,0:T(8,128)(2,1)S(1)}, bf16[8,8,8,128]{3,2,1,0:T(8,128)(2,1)}, u32[]{:S(2)}) copy-start(bf16[8,8,8,128]{3,2,1,0:T(8,128)(2,1)} %fusion.56) | copy-start | bytes 393220
  483.1 3.1 copy-start.7
  483.1 3.1 copy-start.9

commit v2 on v1

--- a/solution.py
+++ b/solution.py
@@ -55,7 +55,7 @@
 
 def gather_kernel(device_count, operand_count, *refs):
     sources, targets = refs[:operand_count], refs[operand_count : 2 * operand_count]
-    own_sem, send_z, recv_z, send_y, recv_y, send_c, recv_c = refs[2 * operand_count :]
+    own_sem, send_up, send_down, recv_z, send_y, recv_y, send_c, recv_c = refs[2 * operand_count :]
     me = lax.axis_index("expert")
     depth = device_count // 4
     place_c, place_y, place_z = lax.rem(me, 2), lax.rem(me // 2, 2), me // 4
@@ -63,25 +63,26 @@
     def index_of(z, y, c):
         return (z * 2 + y) * 2 + c
 
-    partners = [index_of(lax.rem(place_z + k, depth), place_y, place_c) for k in range(1, depth)]
-    origins = [
-        index_of(lax.rem(place_z + depth - k, depth), place_y, place_c) for k in range(depth)
-    ]
-    crossed = [
-        index_of(lax.rem(place_z + depth - k, depth), 1 - place_y, place_c) for k in range(depth)
-    ]
+    upper, lower = index_of(place_z + 1, place_y, place_c), index_of(place_z - 1, place_y, place_c)
     partner_y = index_of(place_z, 1 - place_y, place_c)
     partner_c = index_of(place_z, place_y, 1 - place_c)
-
+    has_upper, has_lower = place_z < depth - 1, place_z > 0
+    operands = range(operand_count)
     barrier = pltpu.get_barrier_semaphore()
-    for peer in partners + [partner_y, partner_c]:
+
+    def greet(peer):
         pl.semaphore_signal(
             barrier, inc=1, device_id={"expert": peer}, device_id_type=pl.DeviceIdType.MESH
         )
-    pl.semaphore_wait(barrier, depth + 1)
-
-    def send(source, target, send_sem, recv_sem, peer):
-        copy = pltpu.make_async_remote_copy(
+
+    for step in (1, depth - 1):
+        greet(index_of(lax.rem(place_z + step, depth), place_y, place_c))
+    greet(partner_y)
+    greet(partner_c)
+    pl.semaphore_wait(barrier, 4)
+
+    def transfer(source, target, send_sem, recv_sem, peer):
+        return pltpu.make_async_remote_copy(
             src_ref=source,
             dst_ref=target,
             send_sem=send_sem,
@@ -89,49 +90,67 @@
             device_id={"expert": peer},
             device_id_type=pl.DeviceIdType.MESH,
         )
-        copy.start()
-        return copy
-
-    owned = []
-    along_z = [[None] * depth for _ in range(operand_count)]
-    along_y = [[None] * depth for _ in range(operand_count)]
-    along_c = [[None] * (2 * depth) for _ in range(operand_count)]
-    for a in range(operand_count):
-        for k in range(1, depth):
-            along_z[a][k] = send(
-                sources[a],
-                targets[a].at[me],
-                send_z.at[a, k],
-                recv_z.at[a, k],
-                partners[k - 1],
+
+    def up(a, origin, source, target):
+        return transfer(source, target, send_up.at[a, origin], recv_z.at[a, origin], upper)
+
+    def down(a, origin, source, target):
+        return transfer(source, target, send_down.at[a, origin], recv_z.at[a, origin], lower)
+
+    def across(a, origin, source, target):
+        return transfer(source, target, send_y.at[a, origin], recv_y.at[a, origin], partner_y)
+
+    def beside(a, slot, source, target):
+        return transfer(source, target, send_c.at[a, slot], recv_c.at[a, slot], partner_c)
+
+    def own_block(a):
+        source, target = sources[a], targets[a].at[me]
+        pl.when(has_upper)(lambda: up(a, place_z, source, target).start())
+        pl.when(has_lower)(lambda: down(a, place_z, source, target).start())
+        across(a, place_z, source, target).start()
+        beside(a, place_z, source, target).start()
+        pltpu.make_async_copy(source, target, own_sem.at[a]).start()
+
+    def relay(a, origin, onward, has_next):
+        block = targets[a].at[index_of(origin, place_y, place_c)]
+        onward(a, origin, block, block).wait_recv()
+        pl.when(has_next)(lambda: onward(a, origin, block, block).start())
+        across(a, origin, block, block).start()
+        beside(a, origin, block, block).start()
+
+    def crossed(a, origin):
+        block = targets[a].at[index_of(origin, 1 - place_y, place_c)]
+        across(a, origin, block, block).wait_recv()
+        beside(a, depth + origin, block, block).start()
+
+    for a in operands:
+        own_block(a)
+    for k in range(1, depth):
+        for a in operands:
+            pl.when(place_z >= k)(lambda: relay(a, place_z - k, up, has_upper))
+            pl.when(place_z + k < depth)(lambda: relay(a, place_z + k, down, has_lower))
+            if k == 1:
+                crossed(a, place_z)
+            else:
+                pl.when(place_z >= k - 1)(lambda: crossed(a, place_z - (k - 1)))
+                pl.when(place_z + k - 1 < depth)(lambda: crossed(a, place_z + (k - 1)))
+    for a in operands:
+        pl.when(place_z >= depth - 1)(lambda: crossed(a, place_z - (depth - 1)))
+        pl.when(place_z + depth - 1 < depth)(lambda: crossed(a, place_z + (depth - 1)))
+    for a in operands:
+        block = sources[a]
+        for slot in range(2 * depth):
+            beside(a, slot, block, targets[a].at[me]).wait_recv()
+            beside(a, slot, block, targets[a].at[me]).wait_send()
+        for origin in range(depth):
+            across(a, origin, block, targets[a].at[me]).wait_send()
+            pl.when(has_upper & (place_z >= origin))(
+                lambda: up(a, origin, block, targets[a].at[me]).wait_send()
             )
-        along_y[a][0] = send(
-            sources[a], targets[a].at[me], send_y.at[a, 0], recv_y.at[a, 0], partner_y
-        )
-        along_c[a][0] = send(
-            sources[a], targets[a].at[me], send_c.at[a, 0], recv_c.at[a, 0], partner_c
-        )
-        owned.append(pltpu.make_async_copy(sources[a], targets[a].at[me], own_sem.at[a]))
-        owned[a].start()
-    for a in range(operand_count):
-        for k in range(1, depth):
-            along_z[a][k].wait_recv()
-            block = targets[a].at[origins[k]]
-            along_y[a][k] = send(block, block, send_y.at[a, k], recv_y.at[a, k], partner_y)
-            along_c[a][k] = send(block, block, send_c.at[a, k], recv_c.at[a, k], partner_c)
-    for a in range(operand_count):
-        for k in range(depth):
-            along_y[a][k].wait_recv()
-            block = targets[a].at[crossed[k]]
-            along_c[a][depth + k] = send(
-                block, block, send_c.at[a, depth + k], recv_c.at[a, depth + k], partner_c
+            pl.when(has_lower & (place_z <= origin))(
+                lambda: down(a, origin, block, targets[a].at[me]).wait_send()
             )
-    for a in range(operand_count):
-        for k in range(2 * depth):
-            along_c[a][k].wait_recv()
-        for copy in along_z[a][1:] + along_y[a] + along_c[a]:
-            copy.wait_send()
-        owned[a].wait()
+        pltpu.make_async_copy(block, targets[a].at[me], own_sem.at[a]).wait()
 
 
 def gather_all(operands, collective_id):
@@ -149,6 +168,7 @@
         out_specs=[pl.BlockSpec(memory_space=pl.ANY)] * operand_count,
         scratch_shapes=[
             pltpu.SemaphoreType.DMA((operand_count,)),
+            pairs,
             pairs,
             pairs,
             pairs,
@@ -255,13 +275,13 @@
 
     def mixture(wide_input, slot_table, combine_table):
         moe_input = rms_scale(wide_input, moe_gain).astype(jnp.bfloat16)
-        (gathered,) = gather_all([jnp.concatenate([moe_input, slot_table], axis=-1)], 1)
-        named = lax.dynamic_slice_in_dim(
-            gathered, model_width + lax.axis_index("expert"), 1, axis=2
-        ).reshape(expert_devices, members, 1, tok_rows)
+        gathered, named = gather_all([moe_input, slot_table], 1)
+        named = lax.dynamic_slice_in_dim(named, lax.axis_index("expert"), 1, axis=2).reshape(
+            expert_devices, members, 1, tok_rows
+        )
         slots = jnp.arange(1, capacity + 1, dtype=jnp.int32).astype(jnp.bfloat16)
         chosen = (named == slots[None, None, :, None]).astype(jnp.bfloat16)
-        source_rows = gathered[:, :, :model_width].reshape(
+        source_rows = gathered.reshape(
             expert_devices, members, tok_rows, model_width
         )
         arrived = jnp.einsum(

time: 489 us -> 417 us (0.85)
  Pallas kernels: 231 us -> 185 us
  local copies, waits for them, and re-layouts: 31.3 us -> 17.1 us
  starting transfers between devices: 36 us -> 26 us
    pallas_call x4, Pallas kernels: 231 us -> 185 us  [gather_all(): pl.pallas_call(functools.partial(gather_kernel, device_count, operand_cou...]
    slice x5 -> x2, local copies, waits for them, and re-layouts: 14.4 us -> 0.2 us  [the longest x3 14.2 us: mixture(): gathered[:, :, :model_width]]
    all_to_all x3, starting transfers between devices: 33 us -> 23 us  [mixture(): lax.all_to_all(produced, 'expert', split_axis=0, concat_axis=0, tiled=True)]
  transfers between devices with their start and end apart: 5 -> 5, of which waited for: 4 -> 4; matrix products, arithmetic and copies ran while one was open for 7% -> 8% of each run, Pallas kernels for 23% -> 21%
where the time goes in v2:
time: 417 us; the launch traced here: 416 us
  Pallas kernels  185 us (44%)
  waiting for transfers between devices  94.2 us (23%)
  matrix products  78 us (19%)
  starting transfers between devices  26 us (6%)
  local copies, waits for them, and re-layouts  17.1 us (4%)
  other arithmetic  15.3 us (4%)
    pallas_call x4, Pallas kernels, gather_all(): pl.pallas_call(functools.partial(gather_kernel, device_count, operand_cou...  185 us
    all_to_all x3, waiting for transfers between devices, mixture(): lax.all_to_all(produced, 'expert', split_axis=0, concat_axis=0, tiled=True)  77.9 us
    all_to_all x3, starting transfers between devices, mixture(): lax.all_to_all(produced, 'expert', split_axis=0, concat_axis=0, tiled=True)  23 us
    dot_general x3, matrix products, expert_rows(): jnp.dot(hidden, down_matrix, preferred_element_type=jnp.float32)  22.9 us
    ppermute x2, waiting for transfers between devices, shifted(): lax.ppermute(value, axis, [(source, source + steps) for source in range(i...  16.4 us
    dot_general x3, matrix products, attend(): jnp.dot(normed, full_mixed, preferred_element_type=jnp.float32)  11.3 us
    dot_general x3, matrix products, attend(): jnp.dot(attended_values, full_out, preferred_element_type=jnp.float32)  10 us
    dot_general x3, matrix products, mixture(): jnp.einsum('nmsi,nmid->nmsd', chosen, source_rows, preferred_element_type...  9.33 us
  transfers between devices with their start and end apart: 5, of which 4 were waited for; matrix products, arithmetic and copies ran while one was open for 8% of the time, Pallas kernels for 21%

profile of v2, /device:TPU:15, one launch (start us, length us, event | category | flops | bytes accessed | tf_op | source)
XLA Modules:
  0.0 416.1 jit_solution(15289824740691271182)
XLA Ops:
  0.0 1.0 copy.57
  1.0 0.7 copy.136
  1.8 2.3 reduce-window.6
  4.9 1.1 multiply_reduce_fusion
  6.1 1.8 fusion.79.refs_0_
  7.9 0.6 dynamic-slice_bitcast_fusion
  8.5 32.3 %shard_map.119 = (bf16[16,64,2048]{2,1,0:T(8,128)(2,1)}, bf16[16,64,128]{2,1,0:T(8,128)(2,1)}) custom-call(bf16[64,2048]{1,0:T(8,128)(2,1)} %fusion.79.refs_0_, bf16[64,128]{1,0:T(8,128)(2,1)} %get-tuple-element.37.refs_1_), custom_call_target="tpu_custom_call" | custom-call | tf_op jit(solution)/shard_map/pallas_call | solution.py:161
  40.9 1.3 dynamic-slice_reduce_fusion.2
  42.2 3.1 convolution_convert_fusion.5
  45.4 1.3 copy-done.4
  46.7 2.8 fusion.16
  49.5 7.6 %convolution_convert_fusion.4 = bf16[512,2048]{1,0:T(8,128)(2,1)} fusion(bf16[1,1,704,2048]{3,2,1,0:T(8,128)(2,1)S(1)} %copy-done, bf16[512,2048]{1,0:T(8,128)(2,1)} %bitcast.315, bf16[1,1,2048,704]{2,3,1,0:T(8,128)(2,1)} %param.20, f32[512,704]{0,1:T(8,128)} %fusion.16), kind=kOutput, calls=%fused_computation.7 | convolution fusion | flops 2956001280 | bytes 11403264 | tf_op jit(solution)/shard_map/dot_general | solution.py:31
  57.1 6.6 %all-to-all-start = ((bf16[16,32,2048]{2,1,0:T(8,128)(2,1)}), bf16[16,32,2048]{2,1,0:T(8,128)(2,1)}, u32[]{:S(2)}, u32[]{:S(2)}) async-start(bf16[16,32,2048]{2,1,0:T(8,128)(2,1)} %bitcast.309), calls=%async_computation | async-start | bytes 4194304 | tf_op jit(solution)/shard_map/all_to_all | solution.py:294
  63.8 0.7 copy.63
  64.5 0.7 multiply_bitcast_fusion
  65.2 0.6 copy.64
  65.8 1.7 pad_maximum_fusion.refs_0_
  67.5 85.8 %shard_map.118 = (bf16[16,128,1280]{2,1,0:T(8,128)(2,1)}, bf16[16,64,2048]{2,1,0:T(8,128)(2,1)}) custom-call(bf16[128,1280]{1,0:T(8,128)(2,1)} %pad_maximum_fusion.refs_0_, bf16[64,2048]{1,0:T(8,128)(2,1)} %bitcast.326), custom_call_target="tpu_custom_call" | custom-call | tf_op jit(solution)/shard_map/pallas_call | solution.py:161
  153.6 4.2 %convolution_convert_fusion.8 = bf16[64,1280]{1,0:T(8,128)(2,1)} fusion(bf16[64,2048]{1,0:T(8,128)(2,1)S(1)} %bitcast.320, bf16[2048,1280]{1,0:T(8,128)(2,1)} %bitcast.300), kind=kOutput, calls=%fused_computation.35 | convolution fusion | flops 335626240 | bytes 5668864 | tf_op jit(solution)/shard_map/dot_general | solution.py:238
  157.7 1.9 fusion.205
  159.7 1.2 fusion.54
  160.9 1.0 select_reduce_fusion
  161.9 0.8 fusion.201
  162.6 3.9 convolution_add_fusion.3
  166.5 2.2 fusion.20
  168.7 1.5 collective-permute-start
  170.2 8.2 %collective-permute-done = bf16[64,2048]{1,0:T(8,128)(2,1)} collective-permute-done((bf16[64,2048]{1,0:T(8,128)(2,1)S(1)}, bf16[64,2048]{1,0:T(8,128)(2,1)}, u32[]{:S(2)}, u32[]{:S(2)}) %collective-permute-start) | collective-permute-done | bytes 262176 | tf_op jit(solution)/shard_map/ppermute | solution.py:16
  178.5 1.1 fusion.74
  179.6 0.5 copy-done.20
  180.2 0.8 fusion.73.refs_0_
  181.0 36.9 %shard_map.120 = (bf16[16,64,2048]{2,1,0:T(8,128)(2,1)}, bf16[16,64,128]{2,1,0:T(8,128)(2,1)}) custom-call(bf16[64,2048]{1,0:T(8,128)(2,1)} %fusion.73.refs_0_, bf16[64,128]{1,0:T(8,128)(2,1)} %get-tuple-element.36.refs_1_), custom_call_target="tpu_custom_call" | custom-call | tf_op jit(solution)/shard_map/pallas_call | solution.py:161
  217.9 1.9 dynamic-slice_reduce_fusion.1
  219.8 1.4 eq.153
  221.2 3.1 convolution_convert_fusion.3
  224.3 1.4 copy-done.5
  225.7 2.8 fusion.14
  228.5 7.6 %convolution_convert_fusion.2 = bf16[512,2048]{1,0:T(8,128)(2,1)} fusion(bf16[1,1,704,2048]{3,2,1,0:T(8,128)(2,1)S(1)} %copy-done, bf16[512,2048]{1,0:T(8,128)(2,1)} %bitcast.317, bf16[1,1,2048,704]{2,3,1,0:T(8,128)(2,1)} %param.20, f32[512,704]{0,1:T(8,128)} %fusion.14), kind=kOutput, calls=%fused_computation.5 | convolution fusion | flops 2956001280 | bytes 11403264 | tf_op jit(solution)/shard_map/dot_general | solution.py:31
  236.1 7.6 %all-to-all-start.1 = ((bf16[16,32,2048]{2,1,0:T(8,128)(2,1)}), bf16[16,32,2048]{2,1,0:T(8,128)(2,1)}, u32[]{:S(2)}, u32[]{:S(2)}) async-start(bf16[16,32,2048]{2,1,0:T(8,128)(2,1)} %bitcast.311), calls=%async_computation.1 | async-start | bytes 4194304 | tf_op jit(solution)/shard_map/all_to_all | solution.py:294
  243.7 0.6 iota_compare_fusion.8
  244.3 0.7 fusion.130
  245.0 3.6 convolution_convert_fusion.7
  248.6 0.7 copy-done.10
  249.2 1.4 fusion.203
  250.6 1.9 fusion.210
  252.5 2.6 fusion.55
  255.1 36.1 %all-to-all-done.1 = bf16[16,32,2048]{2,1,0:T(8,128)(2,1)} async-done(((bf16[16,32,2048]{2,1,0:T(8,128)(2,1)}), bf16[16,32,2048]{2,1,0:T(8,128)(2,1)}, u32[]{:S(2)}, u32[]{:S(2)}) %all-to-all-start.1) | async-done | bytes 2097184 | tf_op jit(solution)/shard_map/all_to_all | solution.py:294
  291.3 2.1 fusion.105
  293.4 3.1 fusion.21
  296.5 1.5 collective-permute-start.1
  298.0 8.1 %collective-permute-done.1 = bf16[64,2048]{1,0:T(8,128)(2,1)S(1)} collective-permute-done((bf16[64,2048]{1,0:T(8,128)(2,1)S(1)}, bf16[64,2048]{1,0:T(8,128)(2,1)S(1)}, u32[]{:S(2)}, u32[]{:S(2)}) %collective-permute-start.1) | collective-permute-done | bytes 262176 | tf_op jit(solution)/shard_map/ppermute | solution.py:16
  306.4 0.8 fusion.71.refs_0_
  307.2 29.9 %shard_map.121 = (bf16[16,64,2048]{2,1,0:T(8,128)(2,1)}, bf16[16,64,128]{2,1,0:T(8,128)(2,1)}) custom-call(bf16[64,2048]{1,0:T(8,128)(2,1)} %fusion.71.refs_0_, bf16[64,128]{1,0:T(8,128)(2,1)} %get-tuple-element.35.refs_1_), custom_call_target="tpu_custom_call" | custom-call | tf_op jit(solution)/shard_map/pallas_call | solution.py:161
  337.2 1.3 dynamic-slice_reduce_fusion
  338.5 3.1 convolution_convert_fusion.1
  341.7 1.4 copy-done.3
  343.1 2.8 fusion.12
  345.9 7.6 %convolution_convert_fusion = bf16[512,2048]{1,0:T(8,128)(2,1)} fusion(bf16[1,1,704,2048]{3,2,1,0:T(8,128)(2,1)S(1)} %copy-done, bf16[512,2048]{1,0:T(8,128)(2,1)} %bitcast.313, bf16[1,1,2048,704]{2,3,1,0:T(8,128)(2,1)} %param.20, f32[512,704]{0,1:T(8,128)} %fusion.12), kind=kOutput, calls=%fused_computation.3 | convolution fusion | flops 2956001280 | bytes 11403264 | tf_op jit(solution)/shard_map/dot_general | solution.py:31
  353.5 8.8 %all-to-all-start.2 = ((bf16[16,32,2048]{2,1,0:T(8,128)(2,1)}), bf16[16,32,2048]{2,1,0:T(8,128)(2,1)}, u32[]{:S(2)}, u32[]{:S(2)}) async-start(bf16[16,32,2048]{2,1,0:T(8,128)(2,1)} %bitcast.310), calls=%async_computation.2 | async-start | bytes 4194304 | tf_op jit(solution)/shard_map/all_to_all | solution.py:294
  362.4 3.6 convolution_convert_fusion.6
  366.4 1.7 fusion.56
  368.1 41.8 %all-to-all-done.2 = bf16[16,32,2048]{2,1,0:T(8,128)(2,1)} async-done(((bf16[16,32,2048]{2,1,0:T(8,128)(2,1)}), bf16[16,32,2048]{2,1,0:T(8,128)(2,1)}, u32[]{:S(2)}, u32[]{:S(2)}) %all-to-all-start.2) | async-done | bytes 2097184 | tf_op jit(solution)/shard_map/all_to_all | solution.py:294
  409.8 2.1 fusion.103
  411.9 3.1 fusion.23
  415.0 1.1 fusion.77
  (81 shorter events, 2.2 us)
Async XLA Ops:
  0.0 49.5 %copy-start = (bf16[1,1,704,2048]{3,2,1,0:T(8,128)(2,1)S(1)}, bf16[1,1,704,2048]{3,2,1,0:T(8,128)(2,1)}, u32[]{:S(2)}) copy-start(bf16[1,1,704,2048]{3,2,1,0:T(8,128)(2,1)} %param.21) | copy-start | bytes 8650756
  1.7 43.7 %copy-start.19 = (bf16[16]{0:T(256)(128)(2,1)}, bf16[16]{0:T(256)(128)(2,1)S(1)}, u32[]{:S(2)}) copy-start(bf16[16]{0:T(256)(128)(2,1)S(1)} %add_convert_fusion) | copy-start | bytes 100
  42.2 4.5 %copy-start.22 = (bf16[1,1,2048,704]{2,3,1,0:T(8,128)(2,1)S(1)}, bf16[1,1,2048,704]{2,3,1,0:T(8,128)(2,1)}, u32[]{:S(2)}) copy-start(bf16[1,1,2048,704]{2,3,1,0:T(8,128)(2,1)} %param.19) | copy-start | bytes 8650756
  45.3 1.4 copy-start.4
  57.1 8.7 %copy-start.15 = (bf16[1,128,128]{2,1,0:T(8,128)(2,1)S(1)}, bf16[1,128,128]{2,1,0:T(8,128)(2,1)}, u32[]{:S(2)}) copy-start(bf16[1,128,128]{2,1,0:T(8,128)(2,1)} %param.17) | copy-start | bytes 98308
  57.1 8.7 %copy-start.16 = (bf16[1,128,128]{2,1,0:T(8,128)(2,1)S(1)}, bf16[1,128,128]{2,1,0:T(8,128)(2,1)}, u32[]{:S(2)}) copy-start(bf16[1,128,128]{2,1,0:T(8,128)(2,1)} %param.16) | copy-start | bytes 98308
  57.1 96.3 %copy-start.1 = (bf16[4,32,2048]{2,1,0:T(8,128)(2,1)S(1)}, bf16[4,32,2048]{2,1,0:T(8,128)(2,1)}, u32[]{:S(2)}) copy-start(bf16[4,32,2048]{2,1,0:T(8,128)(2,1)} %param.12) | copy-start | bytes 1572868
  57.1 96.3 %copy-start.14 = (f32[1,2048]{1,0:T(1,128)S(1)}, f32[1,2048]{1,0:T(1,128)}, u32[]{:S(2)}) copy-start(f32[1,2048]{1,0:T(1,128)} %param.13) | copy-start | bytes 24580
  57.1 109.4 %all-to-all-start = ((bf16[16,32,2048]{2,1,0:T(8,128)(2,1)}), bf16[16,32,2048]{2,1,0:T(8,128)(2,1)}, u32[]{:S(2)}, u32[]{:S(2)}) async-start(bf16[16,32,2048]{2,1,0:T(8,128)(2,1)} %bitcast.309), calls=%async_computation | async-start | bytes 4194304 | tf_op jit(solution)/shard_map/all_to_all | solution.py:294
  166.5 12.0 %copy-start.2 = (bf16[2,32,2048]{2,1,0:T(8,128)(2,1)S(1)}, bf16[2,32,2048]{2,1,0:T(8,128)(2,1)}, u32[]{:S(2)}) copy-start(bf16[2,32,2048]{2,1,0:T(8,128)(2,1)} %get-tuple-element.25) | copy-start | bytes 786436
  166.5 13.7 %copy-start.13 = (f32[1,2048]{1,0:T(1,128)S(1)}, f32[1,2048]{1,0:T(1,128)}, u32[]{:S(2)}) copy-start(f32[1,2048]{1,0:T(1,128)} %param.14) | copy-start | bytes 24580
  168.7 9.7 %copy-start.6 = (bf16[64,2048]{1,0:T(8,128)(2,1)}, bf16[64,2048]{1,0:T(8,128)(2,1)S(1)}, u32[]{:S(2)}) copy-start(bf16[64,2048]{1,0:T(8,128)(2,1)S(1)} %fusion.20) | copy-start | bytes 786436
  168.7 9.7 %collective-permute-start = (bf16[64,2048]{1,0:T(8,128)(2,1)S(1)}, bf16[64,2048]{1,0:T(8,128)(2,1)}, u32[]{:S(2)}, u32[]{:S(2)}) collective-permute-start(bf16[64,2048]{1,0:T(8,128)(2,1)S(1)} %fusion.20), channel_id=1, source_target_pairs={{0,16},{1,17},{2,18},{3,19},{4,20},{5,21},{6,22},{7,23},{8,24},{9,... | collective-permute-start | bytes 786440 | tf_op jit(solution)/shard_map/ppermute | solution.py:16
  179.6 0.5 copy-start.20
  221.2 4.5 %copy-start.23 = (bf16[1,1,2048,704]{2,3,1,0:T(8,128)(2,1)S(1)}, bf16[1,1,2048,704]{2,3,1,0:T(8,128)(2,1)}, u32[]{:S(2)}) copy-start(bf16[1,1,2048,704]{2,3,1,0:T(8,128)(2,1)} %param.19) | copy-start | bytes 8650756
  224.3 1.4 copy-start.5
  236.1 55.1 %all-to-all-start.1 = ((bf16[16,32,2048]{2,1,0:T(8,128)(2,1)}), bf16[16,32,2048]{2,1,0:T(8,128)(2,1)}, u32[]{:S(2)}, u32[]{:S(2)}) async-start(bf16[16,32,2048]{2,1,0:T(8,128)(2,1)} %bitcast.311), calls=%async_computation.1 | async-start | bytes 4194304 | tf_op jit(solution)/shard_map/all_to_all | solution.py:294
  248.5 0.7 copy-start.10
  291.3 2.1 copy-start.12
  296.5 9.9 %copy-start.8 = (bf16[64,2048]{1,0:T(8,128)(2,1)}, bf16[64,2048]{1,0:T(8,128)(2,1)S(1)}, u32[]{:S(2)}) copy-start(bf16[64,2048]{1,0:T(8,128)(2,1)S(1)} %fusion.21) | copy-start | bytes 786436
  296.5 9.6 %collective-permute-start.1 = (bf16[64,2048]{1,0:T(8,128)(2,1)S(1)}, bf16[64,2048]{1,0:T(8,128)(2,1)S(1)}, u32[]{:S(2)}, u32[]{:S(2)}) collective-permute-start(bf16[64,2048]{1,0:T(8,128)(2,1)S(1)} %fusion.21), channel_id=1, source_target_pairs={{0,16},{1,17},{2,18},{3,19},{4,20},{5,21},{6,22},{7,23},{8,24},{9,... | collective-permute-start | bytes 786440 | tf_op jit(solution)/shard_map/ppermute | solution.py:16
  338.5 4.5 %copy-start.24 = (bf16[1,1,2048,704]{2,3,1,0:T(8,128)(2,1)S(1)}, bf16[1,1,2048,704]{2,3,1,0:T(8,128)(2,1)}, u32[]{:S(2)}) copy-start(bf16[1,1,2048,704]{2,3,1,0:T(8,128)(2,1)} %param.19) | copy-start | bytes 8650756
  341.6 1.4 copy-start.3
  353.5 8.8 %copy-start.21 = (pred[128]{0:T(512)(128)(4,1)S(1)}, pred[128]{0:T(512)(128)(4,1)}, u32[]{:S(2)}) copy-start(pred[128]{0:T(512)(128)(4,1)} %get-tuple-element.41) | copy-start | bytes 388
  353.5 56.3 %all-to-all-start.2 = ((bf16[16,32,2048]{2,1,0:T(8,128)(2,1)}), bf16[16,32,2048]{2,1,0:T(8,128)(2,1)}, u32[]{:S(2)}, u32[]{:S(2)}) async-start(bf16[16,32,2048]{2,1,0:T(8,128)(2,1)} %bitcast.310), calls=%async_computation.2 | async-start | bytes 4194304 | tf_op jit(solution)/shard_map/all_to_all | solution.py:294
  362.4 3.6 copy-start.17
  362.4 4.0 copy-start.18
  368.1 43.8 %copy-start.11 = (bf16[8,8,8,128]{3,2,1,0:T(8,128)(2,1)S(1)}, bf16[8,8,8,128]{3,2,1,0:T(8,128)(2,1)}, u32[]{:S(2)}) copy-start(bf16[8,8,8,128]{3,2,1,0:T(8,128)(2,1)} %fusion.56) | copy-start | bytes 393220
  411.9 3.1 copy-start.7
  411.9 3.1 copy-start.9
